TPU v7x, 32 devices: a whole 2x2x4 slice. The times are simulated.
32 devices in a mesh: dp: 4 (over x, core), ctx: 2 (over y), tensor: 4 (over z).
Axes of the slice: x: 2, y: 2, z: 4, core: 2. Of those that a mesh axis runs over, the one named last changes fastest.
Arguments:
- inputs: bfloat16 [2048, 2048], P(('dp', 'ctx'), 'tensor'), may hold values from -6 to 6
- cotangent: bfloat16 [2048, 2048], P(('dp', 'ctx')), may hold values from -6 to 6
- segments: int32 [4, 512], P('dp'), may hold values from 0 to 15, as said below
- positions: int32 [4, 512], P('dp', 'ctx'), may hold values from 0 to 511, as said below
- attention_gain: bfloat16 [2048], replicated, may hold values from 0.5 to 1.5
- query_weight: bfloat16 [2048, 2048], P(None, 'tensor'), may hold values from -0.125 to 0.125
- key_weight: bfloat16 [2048, 1024], P(None, 'tensor'), may hold values from -0.125 to 0.125
- value_weight: bfloat16 [2048, 1024], P(None, 'tensor'), may hold values from -0.125 to 0.125
- query_gain: bfloat16 [128], replicated, may hold values from 0.5 to 1.5
- key_gain: bfloat16 [128], replicated, may hold values from 0.5 to 1.5
- output_weight: bfloat16 [2048, 2048], P('tensor'), may hold values from -0.75 to 0.75
- feed_gain: bfloat16 [2048], replicated, may hold values from 0.3 to 5, as said below
- gate_weight: bfloat16 [2048, 6144], P(None, 'tensor'), may hold values from -0.125 to 0.125
- up_weight: bfloat16 [2048, 6144], P(None, 'tensor'), may hold values from -0.125 to 0.125
- down_weight: bfloat16 [6144, 2048], P('tensor'), may hold values from -0.078125 to 0.078125
Outputs:
- outputs: bfloat16 [2048, 2048], P(('dp', 'ctx'), 'tensor')
- grad_inputs: float32 [2048, 2048], P(('dp', 'ctx'), 'tensor')
- grad_attention_gain: float32 [2048], P('tensor')
- grad_query_weight: float32 [2048, 2048], P(None, 'tensor')
- grad_key_weight: float32 [2048, 1024], P(None, 'tensor')
- grad_value_weight: float32 [2048, 1024], P(None, 'tensor')
- grad_query_gain: float32 [128], replicated
- grad_key_gain: float32 [128], replicated
- grad_output_weight: float32 [2048, 2048], P('tensor')
- grad_feed_gain: float32 [2048], P('tensor')
- grad_gate_weight: float32 [2048, 6144], P(None, 'tensor')
- grad_up_weight: float32 [2048, 6144], P(None, 'tensor')
- grad_down_weight: float32 [6144, 2048], P('tensor')
Inputs may be any that keep to these rules, and one draw needn't show every extreme that they name: `segments`: in each sequence the document numbers start at 0, never fall, and each document is one run of equal numbers; a sequence holds at most 16 documents. `positions`: a token's position counts from 0 at the first token of its document. `feed_gain`: positive gains.
All inputs are finite; a program needn't handle non-finite values.
Results may differ from a plain program's by a relative error of at most 0.024.
Values may be sent and summed in bfloat16 or wider, within the bound.
No kernel may reach another device: no remote copies, remote signals or barrier semaphores. Data moves between devices by JAX's collectives and lax.ppermute only.
A program may use at most 256 MiB of HBM per device.

v0:
```python
import jax
import jax.numpy as jnp
from jax import lax
from jax.sharding import PartitionSpec as P

HD = 128
EPS = 1e-06
THETA = 1000000.0
NEG = -1e30


def rope_tables(position_row):
    half = HD // 2
    freqs = jnp.exp(-(2.0 * jnp.arange(half, dtype=jnp.float32) / HD) * jnp.log(jnp.float32(THETA)))
    angles = position_row.astype(jnp.float32)[:, None] * freqs[None, :]
    return (jnp.cos(angles)[:, None, :], jnp.sin(angles)[:, None, :])


def rotate(value, cosine, sine):
    half = value.shape[-1] // 2
    first = value[..., :half]
    second = value[..., half:]
    return jnp.concatenate(
        [first * cosine - second * sine, second * cosine + first * sine], axis=-1
    )


def head_prepare(raw, gain, cosine, sine):
    count = raw.shape[0]
    heads = raw.reshape(count, -1, HD)
    normed = heads * lax.rsqrt(jnp.mean(heads * heads, axis=-1, keepdims=True) + EPS) * gain
    return rotate(normed, cosine, sine).reshape(count, -1)


def matmul(left, right):
    return jnp.dot(left, right, preferred_element_type=jnp.float32)


def per_device(
    inputs,
    cotangent,
    segments,
    positions,
    attention_gain,
    query_weight,
    key_weight,
    value_weight,
    query_gain,
    key_gain,
    output_weight,
    feed_gain,
    gate_weight,
    up_weight,
    down_weight,
):
    count = inputs.shape[0]
    shard = inputs.shape[1]
    width = cotangent.shape[1]
    column = lax.axis_index("tensor") * shard
    place = lax.axis_index("ctx")
    kv_local = key_weight.shape[1] // HD
    group = query_weight.shape[1] // key_weight.shape[1]
    factor = HD ** (-0.5)
    block = min(512, count)
    blocks = count // block
    gain_one = attention_gain.astype(jnp.float32)
    gain_two = feed_gain.astype(jnp.float32)
    gain_one_part = lax.dynamic_slice_in_dim(gain_one, column, shard)
    gain_two_part = lax.dynamic_slice_in_dim(gain_two, column, shard)
    cosine, sine = rope_tables(positions[0])
    gathered = lax.all_gather(inputs, "tensor", axis=1, tiled=True).astype(jnp.float32)
    inverse_one = lax.rsqrt(jnp.mean(gathered * gathered, axis=-1, keepdims=True) + EPS)
    unit_one = gathered * inverse_one
    normed_one = (unit_one * gain_one).astype(jnp.bfloat16)
    query_raw = matmul(normed_one, query_weight)
    key_raw = matmul(normed_one, key_weight)
    value_rows = matmul(normed_one, value_weight).astype(jnp.bfloat16)
    query_float, query_pull = jax.vjp(
        lambda raw, gain: head_prepare(raw, gain, cosine, sine),
        query_raw,
        query_gain.astype(jnp.float32),
    )
    key_float, key_pull = jax.vjp(
        lambda raw, gain: head_prepare(raw, gain, cosine, sine),
        key_raw,
        key_gain.astype(jnp.float32),
    )
    query_rows = query_float.astype(jnp.bfloat16)
    key_rows = key_float.astype(jnp.bfloat16)
    segment_row = segments[0]
    all_keys, all_values = (
        lax.all_gather(key_rows, "ctx", axis=0, tiled=True),
        lax.all_gather(value_rows, "ctx", axis=0, tiled=True),
    )
    total_keys = all_keys.shape[0]
    key_index = jnp.arange(total_keys, dtype=jnp.int32)
    row_offset = place * count
    key_heads = all_keys.reshape(total_keys, kv_local, HD)
    value_heads = all_values.reshape(total_keys, kv_local, HD)
    query_blocks = query_rows.reshape(blocks, block, kv_local, group, HD)

    def allowed_mask(index):
        start = index * block
        row_index = row_offset + start + jnp.arange(block, dtype=jnp.int32)
        row_segment = lax.dynamic_slice_in_dim(segment_row, row_offset + start, block)
        return (row_segment[:, None] == segment_row[None, :]) & (
            key_index[None, :] <= row_index[:, None]
        )

    def block_scores(rows, index):
        scores = (
            jnp.einsum("qhgd,khd->hgqk", rows, key_heads, preferred_element_type=jnp.float32)
            * factor
        )
        return jnp.where(allowed_mask(index)[None, None], scores, NEG)

    def forward_block(index):
        rows = query_blocks[index]
        scores = block_scores(rows, index)
        top = jnp.max(scores, axis=-1, keepdims=True)
        raised = jnp.exp(scores - top)
        total = jnp.sum(raised, axis=-1, keepdims=True)
        weights = (raised / total).astype(jnp.bfloat16)
        mixed = jnp.einsum(
            "hgqk,khd->qhgd", weights, value_heads, preferred_element_type=jnp.float32
        )
        return (mixed.astype(jnp.bfloat16), top + jnp.log(total))

    mixed_blocks, log_totals = lax.map(forward_block, jnp.arange(blocks, dtype=jnp.int32))
    mixed_rows = mixed_blocks.reshape(count, -1)
    attention_terms = matmul(mixed_rows, output_weight)
    branch = lax.psum_scatter(attention_terms, "tensor", scatter_dimension=1, tiled=True)
    resid_part = (inputs.astype(jnp.float32) + branch).astype(jnp.bfloat16)
    resid_rows = lax.all_gather(resid_part, "tensor", axis=1, tiled=True).astype(jnp.float32)
    inverse_two = lax.rsqrt(jnp.mean(resid_rows * resid_rows, axis=-1, keepdims=True) + EPS)
    unit_two = resid_rows * inverse_two
    normed_two = (unit_two * gain_two).astype(jnp.bfloat16)
    gate = matmul(normed_two, gate_weight)
    up_rows = matmul(normed_two, up_weight)
    sigmoid = jax.nn.sigmoid(gate)
    silu = gate * sigmoid
    hidden = (silu * up_rows).astype(jnp.bfloat16)
    feed = lax.psum_scatter(
        matmul(hidden, down_weight).astype(jnp.bfloat16), "tensor", scatter_dimension=1, tiled=True
    ).astype(jnp.float32)
    outputs = (resid_part.astype(jnp.float32) + feed).astype(jnp.bfloat16)
    grad_down = matmul(hidden.T, cotangent)
    grad_hidden = matmul(cotangent, down_weight.T)
    grad_gate = (grad_hidden * up_rows * sigmoid * (1.0 + gate * (1.0 - sigmoid))).astype(
        jnp.bfloat16
    )
    grad_up = (grad_hidden * silu).astype(jnp.bfloat16)
    grad_gate_w = matmul(normed_two.T, grad_gate)
    grad_up_w = matmul(normed_two.T, grad_up)
    grad_normed_two = matmul(grad_gate, gate_weight.T) + matmul(grad_up, up_weight.T)
    unit_two_part = lax.dynamic_slice_in_dim(unit_two, column, shard, 1)
    grad_out_part = lax.dynamic_slice_in_dim(cotangent, column, shard, 1).astype(jnp.float32)
    grad_two_part = lax.psum_scatter(grad_normed_two, "tensor", scatter_dimension=1, tiled=True)
    row_term_two = jnp.sum(gain_two_part * grad_two_part * unit_two_part, axis=-1)
    row_total_two = lax.psum(row_term_two, "tensor")
    grad_feed_gain = jnp.sum(grad_two_part * unit_two_part, axis=0)
    grad_resid = (
        grad_out_part
        + inverse_two * (gain_two_part * grad_two_part)
        - unit_two_part * (inverse_two / width) * row_total_two[:, None]
    )
    grad_resid_rows = lax.all_gather(grad_resid.astype(jnp.bfloat16), "tensor", axis=1, tiled=True)
    grad_output_w = matmul(mixed_rows.T, grad_resid_rows)
    grad_mixed = matmul(grad_resid_rows, output_weight.T).astype(jnp.bfloat16)
    grad_mixed_blocks = grad_mixed.reshape(blocks, block, kv_local, group, HD)

    def backward_block(carry, index):
        key_total, value_total = carry
        rows = query_blocks[index]
        grad_rows = grad_mixed_blocks[index]
        scores = block_scores(rows, index)
        probs = jnp.exp(scores - log_totals[index])
        grad_probs = jnp.einsum(
            "qhgd,khd->hgqk", grad_rows, value_heads, preferred_element_type=jnp.float32
        )
        delta = jnp.sum(probs * grad_probs, axis=-1, keepdims=True)
        grad_scores = (probs * (grad_probs - delta)).astype(jnp.bfloat16)
        grad_query = (
            jnp.einsum("hgqk,khd->qhgd", grad_scores, key_heads, preferred_element_type=jnp.float32)
            * factor
        )
        key_total = (
            key_total
            + jnp.einsum("hgqk,qhgd->khd", grad_scores, rows, preferred_element_type=jnp.float32)
            * factor
        )
        value_total = value_total + jnp.einsum(
            "hgqk,qhgd->khd",
            probs.astype(jnp.bfloat16),
            grad_rows,
            preferred_element_type=jnp.float32,
        )
        return ((key_total, value_total), grad_query)

    empty = jnp.zeros((total_keys, kv_local, HD), jnp.float32)
    (key_total, value_total), grad_query_blocks = lax.scan(
        backward_block, (empty, empty), jnp.arange(blocks, dtype=jnp.int32)
    )
    grad_query_rows = grad_query_blocks.reshape(count, -1)
    key_total = key_total.reshape(total_keys, -1)
    value_total = value_total.reshape(total_keys, -1)
    grad_key_rot, grad_value = (
        lax.psum_scatter(
            key_total.astype(jnp.bfloat16), "ctx", scatter_dimension=0, tiled=True
        ).astype(jnp.float32),
        lax.psum_scatter(
            value_total.astype(jnp.bfloat16), "ctx", scatter_dimension=0, tiled=True
        ).astype(jnp.float32),
    )
    grad_query_raw, grad_query_gain = query_pull(grad_query_rows)
    grad_key_raw, grad_key_gain = key_pull(grad_key_rot)
    grad_query_low = grad_query_raw.astype(jnp.bfloat16)
    grad_key_low = grad_key_raw.astype(jnp.bfloat16)
    grad_value_low = grad_value.astype(jnp.bfloat16)
    grad_query_w = matmul(normed_one.T, grad_query_low)
    grad_key_w = matmul(normed_one.T, grad_key_low)
    grad_value_w = matmul(normed_one.T, grad_value_low)
    grad_normed_one = (
        matmul(grad_query_low, query_weight.T)
        + matmul(grad_key_low, key_weight.T)
        + matmul(grad_value_low, value_weight.T)
    )
    grad_one_part = lax.psum_scatter(
        grad_normed_one.astype(jnp.bfloat16), "tensor", scatter_dimension=1, tiled=True
    ).astype(jnp.float32)
    unit_one_part = lax.dynamic_slice_in_dim(unit_one, column, shard, 1)
    row_term_one = jnp.sum(gain_one_part * grad_one_part * unit_one_part, axis=-1)
    row_total_one, query_gain_total, key_gain_total = lax.psum(
        (row_term_one, grad_query_gain, grad_key_gain), "tensor"
    )
    grad_inputs = (
        grad_resid
        + inverse_one * (gain_one_part * grad_one_part)
        - unit_one_part * (inverse_one / width) * row_total_one[:, None]
    )
    grad_attention_gain = jnp.sum(grad_one_part * unit_one_part, axis=0)
    summed = (
        lax.psum(grad_attention_gain.astype(jnp.bfloat16), ("dp", "ctx")).astype(jnp.float32),
        lax.psum(grad_query_w.astype(jnp.bfloat16), ("dp", "ctx")).astype(jnp.float32),
        lax.psum(grad_key_w.astype(jnp.bfloat16), ("dp", "ctx")).astype(jnp.float32),
        lax.psum(grad_value_w.astype(jnp.bfloat16), ("dp", "ctx")).astype(jnp.float32),
        lax.psum(query_gain_total.astype(jnp.bfloat16), ("dp", "ctx")).astype(jnp.float32),
        lax.psum(key_gain_total.astype(jnp.bfloat16), ("dp", "ctx")).astype(jnp.float32),
        lax.psum(grad_output_w.astype(jnp.bfloat16), ("dp", "ctx")).astype(jnp.float32),
        lax.psum(grad_feed_gain.astype(jnp.bfloat16), ("dp", "ctx")).astype(jnp.float32),
        lax.psum(grad_gate_w.astype(jnp.bfloat16), ("dp", "ctx")).astype(jnp.float32),
        lax.psum(grad_up_w.astype(jnp.bfloat16), ("dp", "ctx")).astype(jnp.float32),
        lax.psum(grad_down.astype(jnp.bfloat16), ("dp", "ctx")).astype(jnp.float32),
    )
    return (outputs, grad_inputs) + tuple(summed)


def solution(mesh):
    in_specs = (
        P(("dp", "ctx"), "tensor"),
        P(("dp", "ctx"), None),
        P("dp", None),
        P("dp", "ctx"),
        P(),
        P(None, "tensor"),
        P(None, "tensor"),
        P(None, "tensor"),
        P(),
        P(),
        P("tensor", None),
        P(),
        P(None, "tensor"),
        P(None, "tensor"),
        P("tensor", None),
    )
    out_specs = (
        P(("dp", "ctx"), "tensor"),
        P(("dp", "ctx"), "tensor"),
        P("tensor"),
        P(None, "tensor"),
        P(None, "tensor"),
        P(None, "tensor"),
        P(),
        P(),
        P("tensor", None),
        P("tensor"),
        P(None, "tensor"),
        P(None, "tensor"),
        P("tensor", None),
    )
    return jax.shard_map(
        per_device, mesh=mesh, in_specs=in_specs, out_specs=out_specs, check_vma=False
    )
```

profile of v0, /device:TPU:0, one launch (start us, length us, event | category | flops | bytes accessed | tf_op | source)
XLA Modules:
  0.0 697.9 jit_solution(3110859281240040887)
XLA Ops:
  15.3 24.9 %all-gather.4.cloned.1.call-done = bf16[256,2048]{1,0:T(8,128)(2,1)} async-done(((bf16[256,512]{1,0:T(8,128)(2,1)}), bf16[256,2048]{1,0:T(8,128)(2,1)}) %all-gather.4.cloned.1.call-update) | async-done | bytes 1048592 | tf_op jit(solution)/shard_map/all_gather | solution.py:71
  44.4 5.8 all_gather.16
  54.4 5.8 all_gather.17
  70.3 43.7 %reduce-scatter.7.cloned.1.call-done = f32[256,512]{1,0:T(8,128)} async-done(((f32[256,2048]{1,0:T(8,128)}), f32[256,512]{1,0:T(8,128)}) %reduce-scatter.7.cloned.1.call-update) | async-done | bytes 524304 | tf_op jit(solution)/shard_map/reduce_scatter | solution.py:132
  116.3 27.0 %all-gather.6.cloned.1.call-done = bf16[256,2048]{1,0:T(8,128)(2,1)} async-done(((bf16[256,512]{1,0:T(8,128)(2,1)}), bf16[256,2048]{1,0:T(8,128)(2,1)}) %all-gather.6.cloned.1.call-update) | async-done | bytes 1048592 | tf_op jit(solution)/shard_map/all_gather | solution.py:134
  145.6 5.8 fusion.33
  153.4 3.3 multiply_convert_fusion.2
  158.6 3.2 convolution_add_fusion.1
  164.1 41.2 %reduce-scatter.11.cloned.1.call-done = f32[256,512]{1,0:T(8,128)} async-done(((f32[256,2048]{1,0:T(8,128)}), f32[256,512]{1,0:T(8,128)}) %reduce-scatter.11.cloned.1.call-update) | async-done | bytes 524304 | tf_op jit(solution)/shard_map/reduce_scatter | solution.py:158
  207.2 10.5 %psum.105 = f32[256]{0:T(256)} all-reduce(f32[256]{0:T(256)} %get-tuple-element.70), channel_id=1, replica_groups=mesh['dp'=4,'ctx'=2,'tensor'=4] {'tensor'}, use_global_device_ids=true, to_apply=%region_10.11 | all-reduce | flops 256 | bytes 2048 | tf_op jit(solution)/shard_map/psum | solution.py:160
  217.8 2.4 fusion.37
  220.9 25.7 %all-gather.8.cloned.1.call-done = bf16[256,2048]{1,0:T(8,128)(2,1)} async-done(((bf16[256,512]{1,0:T(8,128)(2,1)}), bf16[256,2048]{1,0:T(8,128)(2,1)}) %all-gather.8.cloned.1.call-update) | async-done | bytes 1048592 | tf_op jit(solution)/shard_map/all_gather | solution.py:167
  246.6 2.7 convolution_convert_fusion.8
  251.0 2.4 fusion.4
  256.2 2.2 fusion.12
  258.4 10.1 %reduce-scatter.9.cloned.1.call-start = ((), (), s32[]{:S(2)}) async-start(), calls=%async_computation.9 | async-start | bytes 1310720 | tf_op jit(solution)/shard_map/reduce_scatter | solution.py:143
  268.5 5.9 convolution_convert_fusion.7
  278.4 2.2 multiply_reduce_fusion.1
  288.9 6.1 convolution_convert_fusion
  294.9 4.7 convolution_convert_fusion.1
  299.6 4.7 convolution_convert_fusion.2
  306.3 2.2 convolution_convert_fusion.4
  315.0 25.9 %reduce-scatter.17.cloned.1.call-done = bf16[256,512]{1,0:T(8,128)(2,1)} async-done(((bf16[256,2048]{1,0:T(8,128)(2,1)}), bf16[256,512]{1,0:T(8,128)(2,1)}) %reduce-scatter.17.cloned.1.call-update) | async-done | bytes 262160 | tf_op jit(solution)/shard_map/reduce_scatter | solution.py:228
  342.1 9.7 %all-reduce.4 = (f32[256]{0:T(256)S(1)}, bf16[128]{0:T(256)(128)(2,1)S(1)}, bf16[128]{0:T(256)(128)(2,1)S(1)}) all-reduce(f32[256]{0:T(256)S(1)} %get-tuple-element.72, f32[128]{0:T(128)S(1)} %copy-done.63, f32[128]{0:T(128)S(1)} %copy-done.64), channel_id=1, replica_groups=mesh['dp'=4,'ctx'=2,'tensor'=4] {'tensor'}, use_global_device_ids=true, to_apply=%region_18.19 | all-reduce | flops 512 | bytes 3584 | tf_op jit(solution)/shard_map/psum | solution.py:233
  351.8 14.3 %all-reduce.5 = (bf16[512]{0:T(512)(128)(2,1)S(1)}, bf16[128]{0:T(256)(128)(2,1)S(1)}, bf16[128]{0:T(256)(128)(2,1)S(1)}, bf16[512]{0:T(512)(128)(2,1)S(1)}) all-reduce(bf16[512]{0:T(512)(128)(2,1)S(1)} %get-tuple-element.71, bf16[128]{0:T(256)(128)(2,1)S(1)} %get-tuple-element.78, ...), channel_id=1, replica_groups=mesh['dp'=4,'ctx'=2,'tensor'=4] {'dp','ctx'}, use_global_device_ids=true, to_apply=%region_20.21 | all-reduce | flops 1280 | bytes 5120 | tf_op jit(solution)/shard_map/psum | solution.py:243
  368.3 2.1 fusion.18
  370.4 287.2 %all-reduce.9.cloned.1.call-done = (bf16[2048,512]{1,0:T(8,128)(2,1)}, bf16[2048,256]{1,0:T(8,128)(2,1)}, bf16[2048,256]{1,0:T(8,128)(2,1)}, bf16[512,2048]{1,0:...) async-done(((bf16[2048,512]{1,0:T(8,128)(2,1)}, bf16[2048,256]{1,0:T(8,128)(2,1)}, bf16[2048,256]{1,0:T(8,128)(2,1)}, ...) | async-done | bytes 25165840 | tf_op jit(solution)/shard_map/psum | solution.py:244
  657.6 4.3 convert_element_type.251
  665.8 2.7 convert_element_type.261
  668.4 9.5 %convert_element_type.265 = f32[2048,1536]{1,0:T(8,128)} convert(bf16[2048,1536]{1,0:T(8,128)(2,1)} %get-tuple-element.101) | non-fusion elementwise | flops 3145728 | bytes 18874368 | tf_op jit(solution)/shard_map/convert_element_type | solution.py:251
  677.9 6.6 convert_element_type.267
  684.5 6.3 convert_element_type.269
  (254 shorter events, 72.0 us)
Async XLA Ops:
  7.2 61.0 %copy-start = (bf16[512,2048]{1,0:T(8,128)(2,1)S(1)}, bf16[512,2048]{1,0:T(8,128)(2,1)}, u32[]{:S(2)}) copy-start(bf16[512,2048]{1,0:T(8,128)(2,1)} %param.25) | copy-start | bytes 6291460
  7.2 33.1 %all-gather.4.cloned.1.call-start = ((), (), s32[]{:S(2)}) async-start(), calls=%async_computation.6 | async-start | bytes 1310720 | tf_op jit(solution)/shard_map/all_gather | solution.py:71
  7.9 106.1 %reduce-scatter.7.cloned.1.call-start = ((), (), s32[]{:S(2)}) async-start(), calls=%async_computation.7 | async-start | bytes 2621440 | tf_op jit(solution)/shard_map/reduce_scatter | solution.py:132
  8.6 55.5 %copy-start.58 = (f32[128]{0:T(128)}, f32[128]{0:T(128)S(1)}, u32[]{:S(2)}) copy-start(f32[128]{0:T(128)S(1)} %convert_element_type.215) | copy-start | bytes 1540
  11.2 49.0 %copy-start.56 = (f32[2048]{0:T(1024)}, f32[2048]{0:T(1024)S(1)}, u32[]{:S(2)}) copy-start(f32[2048]{0:T(1024)S(1)} %convert_element_type.208) | copy-start | bytes 24580
  11.7 28.5 %copy-start.16 = (f32[256,64]{1,0:T(8,128)}, f32[256,64]{1,0:T(8,128)S(1)}, u32[]{:S(2)}) copy-start(f32[256,64]{1,0:T(8,128)S(1)} %get-tuple-element.120) | copy-start | bytes 196612
  41.8 9.1 %copy-start.9 = (bf16[256,2048]{1,0:T(8,128)(2,1)S(1)}, bf16[256,2048]{1,0:T(8,128)(2,1)}, u32[]{:S(2)}) copy-start(bf16[256,2048]{1,0:T(8,128)(2,1)} %all-gather.4.cloned.1.call-done) | copy-start | bytes 3145732
  42.3 17.8 %copy-start.50 = (f32[256]{0:T(256)}, f32[256]{0:T(256)S(1)}, u32[]{:S(2)}) copy-start(f32[256]{0:T(256)S(1)} %get-tuple-element.122) | copy-start | bytes 3076
  50.9 9.3 %copy-start.22 = (bf16[2048,512]{1,0:T(8,128)(2,1)S(1)}, bf16[2048,512]{1,0:T(8,128)(2,1)}, u32[]{:S(2)}) copy-start(bf16[2048,512]{1,0:T(8,128)(2,1)} %param.20) | copy-start | bytes 6291460
  53.0 7.2 %copy-start.54 = (f32[256,2]{0,1:T(2,128)}, f32[256,2]{0,1:T(2,128)S(1)}, u32[]{:S(2)}) copy-start(f32[256,2]{0,1:T(2,128)S(1)} %get-tuple-element.125) | copy-start | bytes 6148
  70.2 43.8 %copy-start.30 = (bf16[256,512]{1,0:T(8,128)(2,1)S(1)}, bf16[256,512]{1,0:T(8,128)(2,1)}, u32[]{:S(2)}) copy-start(bf16[256,512]{1,0:T(8,128)(2,1)} %param.15) | copy-start | bytes 786436
  70.2 46.1 %copy-start.52 = (bf16[2048]{0:T(1024)(128)(2,1)S(1)}, bf16[2048]{0:T(1024)(128)(2,1)}, u32[]{:S(2)}) copy-start(bf16[2048]{0:T(1024)(128)(2,1)} %param.26) | copy-start | bytes 12292
  70.3 73.0 %all-gather.6.cloned.1.call-start = ((), (), s32[]{:S(2)}) async-start(), calls=%async_computation.8 | async-start | bytes 1310720 | tf_op jit(solution)/shard_map/all_gather | solution.py:134
  115.9 89.4 %reduce-scatter.11.cloned.1.call-start = ((), (), s32[]{:S(2)}) async-start(), calls=%async_computation.10 | async-start | bytes 2621440 | tf_op jit(solution)/shard_map/reduce_scatter | solution.py:158
  143.3 8.0 %slice-start.4 = ((s8[6291456]{0:T(1024)(128)(4,1)}), s8[4194304]{0:T(1024)(128)(4,1)S(1)}, s32[]{:S(2)}) async-start(s8[6291456]{0:T(1024)(128)(4,1)} %bitcast.132), calls=%async_computation.20 | async-start | bytes 8388608
  143.3 10.0 %slice-start.8 = ((s8[6291456]{0:T(1024)(128)(4,1)}), s8[4194304]{0:T(1024)(128)(4,1)S(1)}, s32[]{:S(2)}) async-start(s8[6291456]{0:T(1024)(128)(4,1)} %bitcast.136), calls=%async_computation.24 | async-start | bytes 8388608
  145.6 7.8 %slice-start.9 = ((s8[6291456]{0:T(1024)(128)(4,1)}), s8[2097152]{0:T(1024)(128)(4,1)S(1)}, s32[]{:S(2)}) async-start(s8[6291456]{0:T(1024)(128)(4,1)} %bitcast.136), calls=%async_computation.25 | async-start | bytes 4194304
  151.4 7.2 %slice-start.6 = ((s8[6291456]{0:T(1024)(128)(4,1)}), s8[4194304]{0:T(1024)(128)(4,1)S(1)}, s32[]{:S(2)}) async-start(s8[6291456]{0:T(1024)(128)(4,1)} %bitcast.134), calls=%async_computation.22 | async-start | bytes 8388608
  161.8 84.8 %all-gather.8.cloned.1.call-start = ((), (), s32[]{:S(2)}) async-start(), calls=%async_computation.11 | async-start | bytes 1310720 | tf_op jit(solution)/shard_map/all_gather | solution.py:167
  220.1 62.4 %reduce-scatter.13.cloned.1.call-start = ((), (), s32[]{:S(2)}) async-start(), calls=%async_computation.12 | async-start | bytes 393216 | tf_op jit(solution)/shard_map/reduce_scatter | solution.py:208
  256.2 28.8 %reduce-scatter.15.cloned.1.call-start = ((), (), s32[]{:S(2)}) async-start(), calls=%async_computation.13 | async-start | bytes 393216 | tf_op jit(solution)/shard_map/reduce_scatter | solution.py:211
  258.4 54.3 %reduce-scatter.9.cloned.1.call-start = ((), (), s32[]{:S(2)}) async-start(), calls=%async_computation.9 | async-start | bytes 1310720 | tf_op jit(solution)/shard_map/reduce_scatter | solution.py:143
  274.4 66.5 %reduce-scatter.17.cloned.1.call-start = ((), (), s32[]{:S(2)}) async-start(), calls=%async_computation.14 | async-start | bytes 1310720 | tf_op jit(solution)/shard_map/reduce_scatter | solution.py:228
  288.8 368.8 %all-reduce.9.cloned.1.call-start = ((), (), s32[]{:S(2)}) async-start(), calls=%async_computation.15 | async-start | bytes 50331648 | tf_op jit(solution)/shard_map/psum | solution.py:244
  312.4 29.6 %copy-start.63 = (f32[128]{0:T(128)S(1)}, f32[128]{0:T(128)}, u32[]{:S(2)}) copy-start(f32[128]{0:T(128)} %get-tuple-element.73) | copy-start | bytes 1540
  312.4 29.6 %copy-start.64 = (f32[128]{0:T(128)S(1)}, f32[128]{0:T(128)}, u32[]{:S(2)}) copy-start(f32[128]{0:T(128)} %get-tuple-element.75) | copy-start | bytes 1540
  312.4 39.4 %copy-start.62 = (bf16[512]{0:T(512)(128)(2,1)S(1)}, bf16[512]{0:T(512)(128)(2,1)}, u32[]{:S(2)}) copy-start(bf16[512]{0:T(512)(128)(2,1)} %get-tuple-element.69) | copy-start | bytes 3076
  312.4 55.9 %copy-start.61 = (f32[256]{0:T(256)S(1)}, f32[256]{0:T(256)}, u32[]{:S(2)}) copy-start(f32[256]{0:T(256)} %get-tuple-element.121) | copy-start | bytes 3076
  665.8 12.2 %slice-start.2 = ((s8[6291456]{0:T(1024)(128)(4,1)}), s8[4194304]{0:T(1024)(128)(4,1)S(1)}, s32[]{:S(2)}) async-start(s8[6291456]{0:T(1024)(128)(4,1)} %bitcast.107), calls=%async_computation.18 | async-start | bytes 8388608
  668.4 9.5 %slice-start.3 = ((s8[6291456]{0:T(1024)(128)(4,1)}), s8[2097152]{0:T(1024)(128)(4,1)S(1)}, s32[]{:S(2)}) async-start(s8[6291456]{0:T(1024)(128)(4,1)} %bitcast.107), calls=%async_computation.19 | async-start | bytes 4194304
  668.4 16.1 %slice-start = ((s8[6291456]{0:T(1024)(128)(4,1)}), s8[4194304]{0:T(1024)(128)(4,1)S(1)}, s32[]{:S(2)}) async-start(s8[6291456]{0:T(1024)(128)(4,1)} %bitcast.105), calls=%async_computation.16 | async-start | bytes 8388608
  677.9 6.6 slice-start.1
  (53 other events, 150.3 us)
Sparse Core Ops, SparseCore 0:
  9.6 30.6 all-gather.3
  70.4 43.6 reduce-scatter.6
  116.0 27.2 all-gather.5
  161.9 43.3 reduce-scatter.10
  220.3 26.2 all-gather.7
  256.3 11.1 reduce-scatter.12
  270.3 11.6 reduce-scatter.14
  284.9 27.1 reduce-scatter.8
  315.1 25.7 reduce-scatter.16
  346.9 310.6 all-reduce.8
where the time goes:
time: 704 us; the launch traced here: 698 us
  waiting for transfers between devices  476 us (68%)
  other arithmetic  67.8 us (10%)
  matrix products  66.3 us (9%)
  blocking collectives  46.1 us (7%)
  between operations  15.3 us (2%)
  local copies, waits for them, and re-layouts  15.1 us (2%)
  starting transfers between devices  10.8 us (2%)
    psum x1, waiting for transfers between devices, per_device(): lax.psum(grad_query_w.astype(jnp.bfloat16), ('dp', 'ctx'))  287 us
    dot_general x21, matrix products, matmul(): return jnp.dot(left, right, preferred_element_type=jnp.float32)  59.2 us
    reduce_scatter x1, waiting for transfers between devices, per_device(): lax.psum_scatter(attention_terms, 'tensor', scatter_dimension=1, tiled=True)  43.7 us
    reduce_scatter x1, waiting for transfers between devices, per_device(): lax.psum_scatter(grad_normed_two, 'tensor', scatter_dimension=1, tiled=True)  41.2 us
    all_gather x1, waiting for transfers between devices, per_device(): lax.all_gather(resid_part, 'tensor', axis=1, tiled=True).astype(jnp.float32)  27 us
    reduce_scatter x1, waiting for transfers between devices, per_device(): lax.psum_scatter(grad_normed_one.astype(jnp.bfloat16), 'tensor', scatter_...  25.9 us
    all_gather x1, waiting for transfers between devices, per_device(): lax.all_gather(grad_resid.astype(jnp.bfloat16), 'tensor', axis=1, tiled=T...  25.7 us
    all_gather x1, waiting for transfers between devices, per_device(): lax.all_gather(inputs, 'tensor', axis=1, tiled=True).astype(jnp.float32)  24.9 us
  transfers between devices with their start and end apart: 10, of which 7 were waited for; matrix products, arithmetic and copies ran while one was open for 9% of the time, Pallas kernels for 0%

commit v1 on v0

--- a/solution.py
+++ b/solution.py
@@ -7,6 +7,11 @@
 EPS = 1e-06
 THETA = 1000000.0
 NEG = -1e30
+
+
+def circles_touch(in_array, axis_key):
+    response = lax.all_gather(in_array, axis_name=axis_key)
+    return jnp.sum(response, 0)
 
 
 def rope_tables(position_row):
@@ -241,7 +246,7 @@
     grad_attention_gain = jnp.sum(grad_one_part * unit_one_part, axis=0)
     summed = (
         lax.psum(grad_attention_gain.astype(jnp.bfloat16), ("dp", "ctx")).astype(jnp.float32),
-        lax.psum(grad_query_w.astype(jnp.bfloat16), ("dp", "ctx")).astype(jnp.float32),
+        circles_touch(grad_query_w.astype(jnp.bfloat16), ("dp", "ctx")).astype(jnp.float32),
         lax.psum(grad_key_w.astype(jnp.bfloat16), ("dp", "ctx")).astype(jnp.float32),
         lax.psum(grad_value_w.astype(jnp.bfloat16), ("dp", "ctx")).astype(jnp.float32),
         lax.psum(query_gain_total.astype(jnp.bfloat16), ("dp", "ctx")).astype(jnp.float32),

time: 704 us -> 755 us (1.072)
  waiting for transfers between devices: 476 us -> 516 us
  other arithmetic: 67.8 us -> 80.8 us
    all_gather x0 -> x1, waiting for transfers between devices: none -> 61.3 us  [circles_touch(): response = lax.all_gather(in_array, axis_name=axis_key)]
    psum x1, waiting for transfers between devices: 287 us -> 264 us  [per_device(): lax.psum(grad_key_w.astype(jnp.bfloat16), ('dp', 'ctx')).astype(jnp.float32)]
    reduce_sum x0 -> x1, other arithmetic: none -> 10.7 us  [circles_touch(): return jnp.sum(response, 0)]
  transfers between devices with their start and end apart: 10 -> 11, of which waited for: 7 -> 8; matrix products, arithmetic and copies ran while one was open for 9% -> 12% of each run, Pallas kernels for 0% -> 0%
where the time goes in v1:
time: 755 us; the launch traced here: 748 us
  waiting for transfers between devices  516 us (68%)
  other arithmetic  80.8 us (11%)
  matrix products  65.6 us (9%)
  blocking collectives  46 us (6%)
  between operations  15 us (2%)
  local copies, waits for them, and re-layouts  14.4 us (2%)
  starting transfers between devices  10.9 us (1%)
    psum x1, waiting for transfers between devices, per_device(): lax.psum(grad_key_w.astype(jnp.bfloat16), ('dp', 'ctx')).astype(jnp.float32)  264 us
    all_gather x1, waiting for transfers between devices, circles_touch(): response = lax.all_gather(in_array, axis_name=axis_key)  61.3 us
    dot_general x21, matrix products, matmul(): return jnp.dot(left, right, preferred_element_type=jnp.float32)  58.5 us
    reduce_scatter x1, waiting for transfers between devices, per_device(): lax.psum_scatter(attention_terms, 'tensor', scatter_dimension=1, tiled=True)  43.8 us
    reduce_scatter x1, waiting for transfers between devices, per_device(): lax.psum_scatter(grad_normed_two, 'tensor', scatter_dimension=1, tiled=True)  41.2 us
    all_gather x1, waiting for transfers between devices, per_device(): lax.all_gather(resid_part, 'tensor', axis=1, tiled=True).astype(jnp.float32)  27 us
    reduce_scatter x1, waiting for transfers between devices, per_device(): lax.psum_scatter(grad_normed_one.astype(jnp.bfloat16), 'tensor', scatter_...  26.4 us
    all_gather x1, waiting for transfers between devices, per_device(): lax.all_gather(grad_resid.astype(jnp.bfloat16), 'tensor', axis=1, tiled=T...  25.6 us
  transfers between devices with their start and end apart: 11, of which 8 were waited for; matrix products, arithmetic and copies ran while one was open for 12% of the time, Pallas kernels for 0%

profile of v1, /device:TPU:0, one launch (start us, length us, event | category | flops | bytes accessed | tf_op | source)
XLA Modules:
  0.0 748.2 jit_solution(1584125095717306505)
XLA Ops:
  15.3 24.9 %all-gather.6.cloned.1.call-done = bf16[256,2048]{1,0:T(8,128)(2,1)} async-done(((bf16[256,512]{1,0:T(8,128)(2,1)}), bf16[256,2048]{1,0:T(8,128)(2,1)}) %all-gather.6.cloned.1.call-update) | async-done | bytes 1048592 | tf_op jit(solution)/shard_map/all_gather | solution.py:76
  44.4 5.8 all_gather.22
  54.4 5.8 all_gather.23
  70.3 43.8 %reduce-scatter.7.cloned.1.call-done = f32[256,512]{1,0:T(8,128)} async-done(((f32[256,2048]{1,0:T(8,128)}), f32[256,512]{1,0:T(8,128)}) %reduce-scatter.7.cloned.1.call-update) | async-done | bytes 524304 | tf_op jit(solution)/shard_map/reduce_scatter | solution.py:137
  116.4 27.0 %all-gather.8.cloned.1.call-done = bf16[256,2048]{1,0:T(8,128)(2,1)} async-done(((bf16[256,512]{1,0:T(8,128)(2,1)}), bf16[256,2048]{1,0:T(8,128)(2,1)}) %all-gather.8.cloned.1.call-update) | async-done | bytes 1048592 | tf_op jit(solution)/shard_map/all_gather | solution.py:139
  145.6 5.1 fusion.33
  152.7 3.3 multiply_convert_fusion.2
  157.9 3.2 convolution_add_fusion.1
  163.4 41.2 %reduce-scatter.11.cloned.1.call-done = f32[256,512]{1,0:T(8,128)} async-done(((f32[256,2048]{1,0:T(8,128)}), f32[256,512]{1,0:T(8,128)}) %reduce-scatter.11.cloned.1.call-update) | async-done | bytes 524304 | tf_op jit(solution)/shard_map/reduce_scatter | solution.py:163
  206.6 10.5 %psum.98 = f32[256]{0:T(256)} all-reduce(f32[256]{0:T(256)} %get-tuple-element.70), channel_id=1, replica_groups=mesh['dp'=4,'ctx'=2,'tensor'=4] {'tensor'}, use_global_device_ids=true, to_apply=%region_10.11 | all-reduce | flops 256 | bytes 2048 | tf_op jit(solution)/shard_map/psum | solution.py:165
  217.1 2.4 fusion.37
  220.3 25.6 %all-gather.10.cloned.1.call-done = bf16[256,2048]{1,0:T(8,128)(2,1)} async-done(((bf16[256,512]{1,0:T(8,128)(2,1)}), bf16[256,2048]{1,0:T(8,128)(2,1)}) %all-gather.10.cloned.1.call-update) | async-done | bytes 1048592 | tf_op jit(solution)/shard_map/all_gather | solution.py:172
  245.9 2.7 convolution_convert_fusion.8
  250.4 2.4 fusion.4
  257.8 10.1 %reduce-scatter.9.cloned.1.call-start = ((), (), s32[]{:S(2)}) async-start(), calls=%async_computation.9 | async-start | bytes 1310720 | tf_op jit(solution)/shard_map/reduce_scatter | solution.py:148
  267.9 5.9 convolution_convert_fusion.7
  277.8 2.2 multiply_reduce_fusion.1
  288.3 6.1 convolution_convert_fusion
  294.3 4.7 convolution_convert_fusion.1
  299.0 4.6 convolution_convert_fusion.2
  313.9 26.4 %reduce-scatter.17.cloned.1.call-done = bf16[256,512]{1,0:T(8,128)(2,1)} async-done(((bf16[256,2048]{1,0:T(8,128)(2,1)}), bf16[256,512]{1,0:T(8,128)(2,1)}) %reduce-scatter.17.cloned.1.call-update) | async-done | bytes 262160 | tf_op jit(solution)/shard_map/reduce_scatter | solution.py:233
  341.4 9.7 %all-reduce.4 = (f32[256]{0:T(256)S(1)}, bf16[128]{0:T(256)(128)(2,1)S(1)}, bf16[128]{0:T(256)(128)(2,1)S(1)}) all-reduce(f32[256]{0:T(256)S(1)} %get-tuple-element.72, f32[128]{0:T(128)S(1)} %copy-done.62, f32[128]{0:T(128)S(1)} %copy-done.63), channel_id=1, replica_groups=mesh['dp'=4,'ctx'=2,'tensor'=4] {'tensor'}, use_global_device_ids=true, to_apply=%region_18.19 | all-reduce | flops 512 | bytes 3584 | tf_op jit(solution)/shard_map/psum | solution.py:238
  351.1 14.2 %all-reduce.5 = (bf16[512]{0:T(512)(128)(2,1)S(1)}, bf16[128]{0:T(256)(128)(2,1)S(1)}, bf16[128]{0:T(256)(128)(2,1)S(1)}, bf16[512]{0:T(512)(128)(2,1)S(1)}) all-reduce(bf16[512]{0:T(512)(128)(2,1)S(1)} %get-tuple-element.71, bf16[128]{0:T(256)(128)(2,1)S(1)} %get-tuple-element.78, ...), channel_id=1, replica_groups=mesh['dp'=4,'ctx'=2,'tensor'=4] {'dp','ctx'}, use_global_device_ids=true, to_apply=%region_20.21 | all-reduce | flops 1280 | bytes 5120 | tf_op jit(solution)/shard_map/psum | solution.py:248
  369.7 264.4 %all-reduce.9.cloned.1.call-done = (bf16[2048,256]{1,0:T(8,128)(2,1)}, bf16[2048,256]{1,0:T(8,128)(2,1)}, bf16[512,2048]{1,0:T(8,128)(2,1)}, bf16[2048,1536]{1,0...) async-done(((bf16[2048,256]{1,0:T(8,128)(2,1)}, bf16[2048,256]{1,0:T(8,128)(2,1)}, bf16[512,2048]{1,0:T(8,128)(2,1)}, bf16[2048,1536]{1,0:T(8,128)(2,1)}, ...) | async-done | bytes 23068688 | tf_op jit(solution)/shard_map/psum | solution.py:250
  634.1 2.8 convert_element_type.255
  639.2 2.7 convert_element_type.263
  641.9 10.5 %convert_element_type.267 = f32[2048,1536]{1,0:T(8,128)} convert(bf16[2048,1536]{1,0:T(8,128)(2,1)} %get-tuple-element.100) | non-fusion elementwise | flops 3145728 | bytes 18874368 | tf_op jit(solution)/shard_map/convert_element_type | solution.py:256
  652.5 6.6 convert_element_type.269
  659.0 6.3 convert_element_type.271
  665.3 61.3 %all-gather.12.cloned.1.call-done = bf16[16384,512]{1,0:T(8,128)(2,1)} async-done(((bf16[2048,512]{1,0:T(8,128)(2,1)}), bf16[16384,512]{1,0:T(8,128)(2,1)}) %all-gather.12.cloned.1.call-update) | async-done | bytes 16777232 | tf_op jit(solution)/shard_map/all_gather | solution.py:13
  726.6 10.7 %reduce_sum.167 = bf16[2048,512]{1,0:T(8,128)(2,1)} reduce(bf16[8,2048,512]{2,1,0:T(8,128)(2,1)} %bitcast.106, bf16[]{:T(256)} %constant.102.clone.1), dimensions={0}, to_apply=%region_21.22 | reduce | flops 7340032 | bytes 18874370 | tf_op jit(solution)/shard_map/reduce_sum | solution.py:14
  737.3 4.2 convert_element_type.253
  (256 shorter events, 76.3 us)
Async XLA Ops:
  7.2 61.0 %copy-start = (bf16[512,2048]{1,0:T(8,128)(2,1)S(1)}, bf16[512,2048]{1,0:T(8,128)(2,1)}, u32[]{:S(2)}) copy-start(bf16[512,2048]{1,0:T(8,128)(2,1)} %param.25) | copy-start | bytes 6291460
  7.2 33.1 %all-gather.6.cloned.1.call-start = ((), (), s32[]{:S(2)}) async-start(), calls=%async_computation.6 | async-start | bytes 1310720 | tf_op jit(solution)/shard_map/all_gather | solution.py:76
  7.9 106.2 %reduce-scatter.7.cloned.1.call-start = ((), (), s32[]{:S(2)}) async-start(), calls=%async_computation.7 | async-start | bytes 2621440 | tf_op jit(solution)/shard_map/reduce_scatter | solution.py:137
  8.6 55.5 %copy-start.57 = (f32[128]{0:T(128)}, f32[128]{0:T(128)S(1)}, u32[]{:S(2)}) copy-start(f32[128]{0:T(128)S(1)} %convert_element_type.217) | copy-start | bytes 1540
  11.2 49.0 %copy-start.55 = (f32[2048]{0:T(1024)}, f32[2048]{0:T(1024)S(1)}, u32[]{:S(2)}) copy-start(f32[2048]{0:T(1024)S(1)} %convert_element_type.210) | copy-start | bytes 24580
  11.7 28.5 %copy-start.16 = (f32[256,64]{1,0:T(8,128)}, f32[256,64]{1,0:T(8,128)S(1)}, u32[]{:S(2)}) copy-start(f32[256,64]{1,0:T(8,128)S(1)} %get-tuple-element.119) | copy-start | bytes 196612
  41.8 9.2 %copy-start.9 = (bf16[256,2048]{1,0:T(8,128)(2,1)S(1)}, bf16[256,2048]{1,0:T(8,128)(2,1)}, u32[]{:S(2)}) copy-start(bf16[256,2048]{1,0:T(8,128)(2,1)} %all-gather.6.cloned.1.call-done) | copy-start | bytes 3145732
  42.3 17.8 %copy-start.49 = (f32[256]{0:T(256)}, f32[256]{0:T(256)S(1)}, u32[]{:S(2)}) copy-start(f32[256]{0:T(256)S(1)} %get-tuple-element.121) | copy-start | bytes 3076
  50.9 9.3 %copy-start.22 = (bf16[2048,512]{1,0:T(8,128)(2,1)S(1)}, bf16[2048,512]{1,0:T(8,128)(2,1)}, u32[]{:S(2)}) copy-start(bf16[2048,512]{1,0:T(8,128)(2,1)} %param.20) | copy-start | bytes 6291460
  53.0 7.2 copy-start.53
  70.3 43.8 %copy-start.29 = (bf16[256,512]{1,0:T(8,128)(2,1)S(1)}, bf16[256,512]{1,0:T(8,128)(2,1)}, u32[]{:S(2)}) copy-start(bf16[256,512]{1,0:T(8,128)(2,1)} %param.15) | copy-start | bytes 786436
  70.3 46.1 %copy-start.51 = (bf16[2048]{0:T(1024)(128)(2,1)S(1)}, bf16[2048]{0:T(1024)(128)(2,1)}, u32[]{:S(2)}) copy-start(bf16[2048]{0:T(1024)(128)(2,1)} %param.26) | copy-start | bytes 12292
  70.3 73.1 %all-gather.8.cloned.1.call-start = ((), (), s32[]{:S(2)}) async-start(), calls=%async_computation.8 | async-start | bytes 1310720 | tf_op jit(solution)/shard_map/all_gather | solution.py:139
  115.9 88.7 %reduce-scatter.11.cloned.1.call-start = ((), (), s32[]{:S(2)}) async-start(), calls=%async_computation.10 | async-start | bytes 2621440 | tf_op jit(solution)/shard_map/reduce_scatter | solution.py:163
  143.4 7.3 slice-start.4
  145.6 7.1 slice-start.8
  150.7 7.1 slice-start.6
  161.1 84.8 %all-gather.10.cloned.1.call-start = ((), (), s32[]{:S(2)}) async-start(), calls=%async_computation.11 | async-start | bytes 1310720 | tf_op jit(solution)/shard_map/all_gather | solution.py:172
  219.5 62.4 %reduce-scatter.13.cloned.1.call-start = ((), (), s32[]{:S(2)}) async-start(), calls=%async_computation.12 | async-start | bytes 393216 | tf_op jit(solution)/shard_map/reduce_scatter | solution.py:213
  255.5 28.8 %reduce-scatter.15.cloned.1.call-start = ((), (), s32[]{:S(2)}) async-start(), calls=%async_computation.13 | async-start | bytes 393216 | tf_op jit(solution)/shard_map/reduce_scatter | solution.py:216
  257.8 53.8 %reduce-scatter.9.cloned.1.call-start = ((), (), s32[]{:S(2)}) async-start(), calls=%async_computation.9 | async-start | bytes 1310720 | tf_op jit(solution)/shard_map/reduce_scatter | solution.py:148
  273.8 66.4 %reduce-scatter.17.cloned.1.call-start = ((), (), s32[]{:S(2)}) async-start(), calls=%async_computation.14 | async-start | bytes 1310720 | tf_op jit(solution)/shard_map/reduce_scatter | solution.py:233
  288.2 345.9 %all-reduce.9.cloned.1.call-start = ((), (), s32[]{:S(2)}) async-start(), calls=%async_computation.16 | async-start | bytes 46137344 | tf_op jit(solution)/shard_map/psum | solution.py:250
  308.9 417.7 %all-gather.12.cloned.1.call-start = ((), (), s32[]{:S(2)}) async-start(), calls=%async_computation.15 | async-start | bytes 18874368 | tf_op jit(solution)/shard_map/all_gather | solution.py:13
  311.3 30.1 %copy-start.62 = (f32[128]{0:T(128)S(1)}, f32[128]{0:T(128)}, u32[]{:S(2)}) copy-start(f32[128]{0:T(128)} %get-tuple-element.73) | copy-start | bytes 1540
  311.3 30.1 %copy-start.63 = (f32[128]{0:T(128)S(1)}, f32[128]{0:T(128)}, u32[]{:S(2)}) copy-start(f32[128]{0:T(128)} %get-tuple-element.75) | copy-start | bytes 1540
  311.3 39.8 %copy-start.61 = (bf16[512]{0:T(512)(128)(2,1)S(1)}, bf16[512]{0:T(512)(128)(2,1)}, u32[]{:S(2)}) copy-start(bf16[512]{0:T(512)(128)(2,1)} %get-tuple-element.69) | copy-start | bytes 3076
  311.3 56.2 %copy-start.60 = (f32[256]{0:T(256)S(1)}, f32[256]{0:T(256)}, u32[]{:S(2)}) copy-start(f32[256]{0:T(256)} %get-tuple-element.120) | copy-start | bytes 3076
  639.2 13.2 %slice-start.2 = ((s8[6291456]{0:T(1024)(128)(4,1)}), s8[4194304]{0:T(1024)(128)(4,1)S(1)}, s32[]{:S(2)}) async-start(s8[6291456]{0:T(1024)(128)(4,1)} %bitcast.109), calls=%async_computation.19 | async-start | bytes 8388608
  641.9 10.5 %slice-start.3 = ((s8[6291456]{0:T(1024)(128)(4,1)}), s8[2097152]{0:T(1024)(128)(4,1)S(1)}, s32[]{:S(2)}) async-start(s8[6291456]{0:T(1024)(128)(4,1)} %bitcast.109), calls=%async_computation.20 | async-start | bytes 4194304
  641.9 17.1 %slice-start = ((s8[6291456]{0:T(1024)(128)(4,1)}), s8[4194304]{0:T(1024)(128)(4,1)S(1)}, s32[]{:S(2)}) async-start(s8[6291456]{0:T(1024)(128)(4,1)} %bitcast.107), calls=%async_computation.17 | async-start | bytes 8388608
  726.6 14.9 %copy-start.1 = (bf16[512,2048]{1,0:T(8,128)(2,1)S(1)}, bf16[512,2048]{1,0:T(8,128)(2,1)}, u32[]{:S(2)}) copy-start(bf16[512,2048]{1,0:T(8,128)(2,1)} %param.25) | copy-start | bytes 6291460
  (53 other events, 149.6 us)
Sparse Core Ops, SparseCore 0:
  9.6 30.6 all-gather.5
  70.4 43.6 reduce-scatter.6
  116.1 27.2 all-gather.7
  161.2 43.3 reduce-scatter.10
  219.6 26.2 all-gather.9
  255.7 11.1 reduce-scatter.12
  269.7 11.6 reduce-scatter.14
  284.3 27.1 reduce-scatter.8
  314.4 25.7 reduce-scatter.16
  346.1 287.9 all-reduce.8
  636.7 89.8 all-gather.11
